TPU v7x, 32 devices: a whole 2x2x4 slice. The times are simulated.
32 devices in a mesh: dp: 16 (over z, x, core), tensor: 2 (over y).
Axes of the slice: x: 2, y: 2, z: 4, core: 2. Of those that a mesh axis runs over, the one named last changes fastest.
Arguments:
- tokens: bfloat16 [4096, 8192], P('dp', 'tensor'), may hold values from -6 to 6
- out_grad: bfloat16 [4096, 2, 256], P('dp', 'tensor'), may hold values from -2 to 2
- active: int32 [16, 2, 2], P('dp', 'tensor'), may hold values from 0 to 112, as said below
- w_gate: bfloat16 [8192, 28672], P('dp', 'tensor'), may hold values from -0.0625 to 0.0625
- w_up: bfloat16 [8192, 28672], P('dp', 'tensor'), may hold values from -0.0625 to 0.0625
Outputs:
- input_grad: bfloat16 [4096, 8192], P('dp', 'tensor')
- gate_weight_grad: bfloat16 [8192, 28672], P('dp', 'tensor')
- up_weight_grad: bfloat16 [8192, 28672], P('dp', 'tensor')
Inputs may be any that keep to these rules, and one draw needn't show every extreme that they name: `active`: each entry is a block number of the shard or 112 for an empty slot. In every tile and shard the live entries come first, are distinct and number at least one; in every tile some shard has all 2 slots live.
All inputs are finite; a program needn't handle non-finite values.
Results may differ from a plain program's by a relative error of at most 0.014.
Values may be sent and summed in bfloat16 or wider, within the bound.
No kernel may reach another device: no remote copies, remote signals or barrier semaphores. Data moves between devices by JAX's collectives and lax.ppermute only.
A program may use at most 128 MiB of HBM per device.

v0:
```python
import jax
import jax.numpy as jnp
from jax import lax
from jax.sharding import PartitionSpec as P

BLOCK = 128
TILE = 256
CAP = 2


def per_device(tokens, out_grad, active, w_gate, w_up):
    row_count = tokens.shape[0]
    tiles_here = active.shape[0]
    blocks = w_gate.shape[1] // BLOCK
    rows_local = w_gate.shape[0]
    gathered = lax.all_gather(tokens, "tensor", axis=1, tiled=True)
    full_width = gathered.shape[1]
    listed = lax.all_gather(active, "dp", axis=0, tiled=True)
    peer_count = lax.axis_size("dp")
    slot_count = tiles_here * CAP
    wanted = jnp.minimum(listed.reshape(peer_count, slot_count), blocks - 1)
    gate_send = jnp.take(w_gate.reshape(rows_local, blocks, BLOCK), wanted, axis=1).reshape(
        rows_local, peer_count, slot_count * BLOCK
    )
    up_send = jnp.take(w_up.reshape(rows_local, blocks, BLOCK), wanted, axis=1).reshape(
        rows_local, peer_count, slot_count * BLOCK
    )
    gate_cols, up_cols = (
        lax.all_to_all(gate_send, "dp", split_axis=1, concat_axis=0, tiled=True),
        lax.all_to_all(up_send, "dp", split_axis=1, concat_axis=0, tiled=True),
    )
    tile_tokens = gathered.reshape(tiles_here, TILE, full_width)
    gate_value = jnp.einsum(
        "tnd,dtc->tnc", tile_tokens, gate_cols, preferred_element_type=jnp.float32
    )
    up_value = jnp.einsum("tnd,dtc->tnc", tile_tokens, up_cols, preferred_element_type=jnp.float32)
    alive = (active.reshape(tiles_here, 1, CAP, 1) < blocks).astype(jnp.float32)
    alive_mask = jnp.broadcast_to(alive, (tiles_here, 1, CAP, BLOCK)).reshape(
        tiles_here, 1, CAP * BLOCK
    )
    upstream = out_grad.reshape(tiles_here, TILE, CAP * BLOCK).astype(jnp.float32)
    positive = jnp.maximum(gate_value, 0.0)
    gate_grad = (upstream * up_value * 2.0 * positive * alive_mask).astype(jnp.bfloat16)
    up_grad = (upstream * positive * positive * alive_mask).astype(jnp.bfloat16)
    partial_value = jnp.einsum(
        "tnc,dtc->tnd", gate_grad, gate_cols, preferred_element_type=jnp.float32
    )
    partial_value = partial_value + jnp.einsum(
        "tnc,dtc->tnd", up_grad, up_cols, preferred_element_type=jnp.float32
    )
    summed = lax.psum_scatter(
        partial_value.reshape(row_count, full_width).astype(jnp.bfloat16),
        "tensor",
        scatter_dimension=1,
        tiled=True,
    )
    row_slices = lax.all_to_all(gathered, "dp", split_axis=1, concat_axis=0, tiled=True)
    slices_tiled = row_slices.reshape(peer_count * tiles_here, TILE, rows_local)
    gate_all, up_all = (
        lax.all_gather(gate_grad, "dp", axis=0, tiled=True),
        lax.all_gather(up_grad, "dp", axis=0, tiled=True),
    )
    gate_terms = jnp.einsum(
        "tnr,tnc->rtc", slices_tiled, gate_all, preferred_element_type=jnp.float32
    ).astype(jnp.bfloat16)
    up_terms = jnp.einsum(
        "tnr,tnc->rtc", slices_tiled, up_all, preferred_element_type=jnp.float32
    ).astype(jnp.bfloat16)
    gate_terms = gate_terms.reshape(rows_local, peer_count * slot_count, BLOCK)
    up_terms = up_terms.reshape(rows_local, peer_count * slot_count, BLOCK)
    placing = (
        listed.reshape(peer_count * slot_count, 1) == jnp.arange(blocks, dtype=jnp.int32)[None, :]
    ).astype(jnp.bfloat16)
    gate_weight_grad = jnp.einsum(
        "rsk,sb->rbk", gate_terms, placing, preferred_element_type=jnp.float32
    )
    up_weight_grad = jnp.einsum(
        "rsk,sb->rbk", up_terms, placing, preferred_element_type=jnp.float32
    )
    gate_weight_grad = gate_weight_grad.reshape(rows_local, blocks * BLOCK).astype(jnp.bfloat16)
    up_weight_grad = up_weight_grad.reshape(rows_local, blocks * BLOCK).astype(jnp.bfloat16)
    return (summed, gate_weight_grad, up_weight_grad)


def solution(mesh):
    placed = (
        P("dp", "tensor"),
        P("dp", "tensor", None),
        P("dp", "tensor", None),
        P("dp", "tensor"),
        P("dp", "tensor"),
    )
    return jax.shard_map(
        per_device,
        mesh=mesh,
        in_specs=placed,
        out_specs=(P("dp", "tensor"), P("dp", "tensor"), P("dp", "tensor")),
        check_vma=False,
    )
```

profile of v0, /device:TPU:0, one launch (start us, length us, event | category | flops | bytes accessed | tf_op | source)
XLA Modules:
  0.0 549.0 jit_solution(14331622517996536747)
XLA Ops:
  7.2 23.3 %all_gather.12 = s32[16,1,2]{2,1,0:T(1,128)S(1)} all-gather(s32[1,1,2]{2,1,0:T(1,128)} %param.9), channel_id=1, replica_groups=mesh['dp'=16,'tensor'=2] {'dp'}, dimensions={0}, use_global_device_ids=true | all-gather | bytes 136 | tf_op jit(solution)/shard_map/all_gather | solution.py:18
  30.8 19.9 %copy.77 = bf16[512,14336]{0,1:T(8,128)(2,1)} copy(bf16[512,14336]{1,0:T(8,128)(2,1)} %param.10) | data formatting | bytes 29360128 | tf_op args[3]
  50.8 19.9 %copy.79 = bf16[512,112,128]{2,0,1:T(8,128)(2,1)} copy(bf16[512,112,128]{0,2,1:T(8,128)(2,1)} %bitcast.100) | data formatting | bytes 29360128 | tf_op jit(solution)/shard_map/reshape | solution.py:22
  70.7 19.9 %copy.71 = bf16[512,14336]{0,1:T(8,128)(2,1)} copy(bf16[512,14336]{1,0:T(8,128)(2,1)} %param.11) | data formatting | bytes 29360128 | tf_op args[4]
  90.6 19.9 %copy.73 = bf16[512,112,128]{2,0,1:T(8,128)(2,1)} copy(bf16[512,112,128]{0,2,1:T(8,128)(2,1)} %bitcast.101) | data formatting | bytes 29360128 | tf_op jit(solution)/shard_map/reshape | solution.py:25
  110.5 8.2 %gather_fusion.1 = bf16[32,512,128]{2,1,0:T(8,128)(2,1)} fusion(bf16[512,112,128]{2,0,1:T(8,128)(2,1)} %copy.79, s32[1024]{0:T(1024)S(1)} %pad_clamp_fusion), kind=kCustom, calls=%fused_computation.1.clone | custom fusion | bytes 8388736 | tf_op jit(solution)/shard_map/jit(_take)/gather | solution.py:22
  118.7 8.3 %gather_fusion = bf16[32,512,128]{2,1,0:T(8,128)(2,1)} fusion(bf16[512,112,128]{2,0,1:T(8,128)(2,1)} %copy.73, s32[1024]{0:T(1024)S(1)} %pad_clamp_fusion), kind=kCustom, calls=%fused_computation.clone | custom fusion | bytes 8388736 | tf_op jit(solution)/shard_map/jit(_take)/gather | solution.py:25
  127.0 5.2 select_bitcast_fusion.1
  132.2 2.8 copy.106
  135.0 4.5 all-to-all-start.1
  139.5 4.9 copy.107
  144.4 72.6 %all-to-all-done.1 = bf16[512,16,256]{2,0,1:T(8,128)(2,1)} async-done(((bf16[512,16,256]{2,0,1:T(8,128)(2,1)}), bf16[512,16,256]{2,0,1:T(8,128)(2,1)}, u32[]{:S(2)}, u32[]{:S(2)}) %all-to-all-start.1) | async-done | bytes 4194336 | tf_op jit(solution)/shard_map/all_to_all | solution.py:29
  217.0 19.8 %all-to-all-start = ((bf16[512,16,256]{2,0,1:T(8,128)(2,1)}), bf16[512,16,256]{2,0,1:T(8,128)(2,1)}, u32[]{:S(2)}, u32[]{:S(2)}) async-start(bf16[512,16,256]{2,0,1:T(8,128)(2,1)} %bitcast.107), calls=%async_computation | async-start | bytes 8388608 | tf_op jit(solution)/shard_map/all_to_all | solution.py:30
  239.6 58.2 %all-gather.6.cloned.1.call-done = bf16[256,8192]{0,1:T(8,128)(2,1)} async-done(((bf16[256,4096]{0,1:T(8,128)(2,1)}), bf16[256,8192]{0,1:T(8,128)(2,1)}) %all-gather.6.cloned.1.call-update) | async-done | bytes 4194320 | tf_op jit(solution)/shard_map/all_gather | solution.py:16
  297.8 5.4 fusion.22
  303.2 11.1 %all-to-all-done = bf16[512,16,256]{2,0,1:T(8,128)(2,1)} async-done(((bf16[512,16,256]{2,0,1:T(8,128)(2,1)}), bf16[512,16,256]{2,0,1:T(8,128)(2,1)}, u32[]{:S(2)}, u32[]{:S(2)}) %all-to-all-start) | async-done | bytes 4194336 | tf_op jit(solution)/shard_map/all_to_all | solution.py:30
  314.4 5.4 fusion.20
  320.5 6.4 %copy.81 = bf16[256,16,512]{2,0,1:T(8,128)(2,1)} copy(bf16[256,16,512]{0,2,1:T(8,128)(2,1)} %bitcast.104) | data formatting | bytes 8388608 | tf_op jit(solution)/shard_map/all_to_all | solution.py:57
  327.0 19.8 %all-to-all-start.2 = ((bf16[256,16,512]{2,0,1:T(8,128)(2,1)}), bf16[256,16,512]{2,0,1:T(8,128)(2,1)}, u32[]{:S(2)}, u32[]{:S(2)}) async-start(bf16[256,16,512]{2,0,1:T(8,128)(2,1)} %copy.81), calls=%async_computation.3 | async-start | bytes 8388608 | tf_op jit(solution)/shard_map/all_to_all | solution.py:57
  347.0 3.5 fusion.29
  350.6 5.6 %fusion = bf16[256,8192]{1,0:T(8,128)(2,1)} fusion(f32[256,8192]{1,0:T(8,128)S(1)} %fusion.29, bf16[256,256]{0,1:T(8,128)(2,1)S(1)} %copy-done.3, bf16[8192,256]{1,0:T(8,128)(2,1)} %bitcast.7), kind=kOutput, calls=%fused_computation.7 | convolution fusion | flops 1077936128 | bytes 16908288 | tf_op jit(solution)/shard_map/tnc,dtc->tnd/dot_general | solution.py:48
  357.5 65.8 %all-gather.8.cloned.1.call-done = bf16[4096,256]{0,1:T(8,128)(2,1)} async-done(((bf16[256,256]{0,1:T(8,128)(2,1)}), bf16[4096,256]{0,1:T(8,128)(2,1)}) %all-gather.8.cloned.1.call-update) | async-done | bytes 2097168 | tf_op jit(solution)/shard_map/all_gather | solution.py:60
  423.3 11.5 %all-to-all-done.2 = bf16[256,16,512]{2,0,1:T(8,128)(2,1)} async-done(((bf16[256,16,512]{2,0,1:T(8,128)(2,1)}), bf16[256,16,512]{2,0,1:T(8,128)(2,1)}, u32[]{:S(2)}, u32[]{:S(2)}) %all-to-all-start.2) | async-done | bytes 4194336 | tf_op jit(solution)/shard_map/all_to_all | solution.py:57
  434.9 6.1 %fusion.5 = bf16[16,256,512]{2,1,0:T(8,128)(2,1)} fusion(bf16[256,16,512]{2,0,1:T(8,128)(2,1)} %all-to-all-done.2, bf16[32,16,8,256]{3,2,1,0:T(8,128)(2,1)} %bitcast.113), kind=kOutput, calls=%fused_computation.16 | convolution fusion | flops 1075838976 | bytes 10485760 | tf_op jit(solution)/shard_map/tnr,tnc->rtc/dot_general | solution.py:63
  441.0 7.9 %copy.83 = bf16[512,32,128]{2,1,0:T(8,128)(2,1)} copy(bf16[512,32,128]{0,2,1:T(8,128)(2,1)} %bitcast.110) | data formatting | bytes 8388608 | tf_op jit(solution)/shard_map/reshape | solution.py:69
  448.9 27.4 %all-gather.10.cloned.1.call-done = bf16[4096,256]{0,1:T(8,128)(2,1)} async-done(((bf16[256,256]{0,1:T(8,128)(2,1)}), bf16[4096,256]{0,1:T(8,128)(2,1)}) %all-gather.10.cloned.1.call-update) | async-done | bytes 2097168 | tf_op jit(solution)/shard_map/all_gather | solution.py:61
  476.3 6.1 %fusion.8 = bf16[16,256,512]{2,1,0:T(8,128)(2,1)} fusion(bf16[256,16,512]{2,0,1:T(8,128)(2,1)} %all-to-all-done.2, bf16[32,16,8,256]{3,2,1,0:T(8,128)(2,1)} %bitcast.114), kind=kOutput, calls=%fused_computation.17 | convolution fusion | flops 1075838976 | bytes 10485760 | tf_op jit(solution)/shard_map/tnr,tnc->rtc/dot_general | solution.py:66
  482.4 8.0 %copy.85 = bf16[512,32,128]{2,1,0:T(8,128)(2,1)} copy(bf16[512,32,128]{0,2,1:T(8,128)(2,1)} %bitcast.109) | data formatting | bytes 8388608 | tf_op jit(solution)/shard_map/reshape | solution.py:70
  490.4 11.7 %convolution_convert_fusion = bf16[112,512,128]{2,0,1:T(8,128)(2,1)} fusion(bf16[512,32,128]{2,1,0:T(8,128)(2,1)} %copy.85, s32[32]{0:T(128)S(1)} %eq.15), kind=kOutput, calls=%fused_computation.5 | convolution fusion | flops 477105664 | bytes 18874496 | tf_op jit(solution)/shard_map/rsk,sb->rbk/dot_general | solution.py:77
  502.1 16.6 %copy.104 = bf16[64,8,112,128]{3,1,2,0:T(8,128)(2,1)} copy(bf16[64,8,112,128]{3,2,1,0:T(8,128)(2,1)} %bitcast.103) | data formatting | bytes 29360128
  518.7 7.4 %convolution_convert_fusion.1 = bf16[112,512,128]{2,0,1:T(8,128)(2,1)} fusion(bf16[512,32,128]{2,1,0:T(8,128)(2,1)S(1)} %copy-done, s32[32]{0:T(128)S(1)} %eq.15), kind=kOutput, calls=%fused_computation.6 | convolution fusion | flops 477105664 | bytes 18874496 | tf_op jit(solution)/shard_map/rsk,sb->rbk/dot_general | solution.py:74
  526.1 16.4 %copy.105 = bf16[64,8,112,128]{3,1,2,0:T(8,128)(2,1)} copy(bf16[64,8,112,128]{3,2,1,0:T(8,128)(2,1)} %bitcast.102) | data formatting | bytes 29360128
  (35 shorter events, 5.4 us)
Async XLA Ops:
  135.0 82.0 %all-to-all-start.1 = ((bf16[512,16,256]{2,0,1:T(8,128)(2,1)}), bf16[512,16,256]{2,0,1:T(8,128)(2,1)}, u32[]{:S(2)}, u32[]{:S(2)}) async-start(bf16[512,16,256]{2,0,1:T(8,128)(2,1)} %bitcast.108), calls=%async_computation.1 | async-start | bytes 8388608 | tf_op jit(solution)/shard_map/all_to_all | solution.py:29
  217.0 19.9 %copy-start.1 = (bf16[256,4096]{1,0:T(8,128)(2,1)S(1)}, bf16[256,4096]{1,0:T(8,128)(2,1)}, u32[]{:S(2)}) copy-start(bf16[256,4096]{1,0:T(8,128)(2,1)} %param.7) | copy-start | bytes 6291460
  217.0 97.3 %all-to-all-start = ((bf16[512,16,256]{2,0,1:T(8,128)(2,1)}), bf16[512,16,256]{2,0,1:T(8,128)(2,1)}, u32[]{:S(2)}, u32[]{:S(2)}) async-start(bf16[512,16,256]{2,0,1:T(8,128)(2,1)} %bitcast.107), calls=%async_computation | async-start | bytes 8388608 | tf_op jit(solution)/shard_map/all_to_all | solution.py:30
  236.8 2.6 copy-start.4
  236.8 2.7 copy-start.5
  236.8 61.0 %all-gather.6.cloned.1.call-start = ((), (), s32[]{:S(2)}) async-start(), calls=%async_computation.4 | async-start | bytes 6291456 | tf_op jit(solution)/shard_map/all_gather | solution.py:16
  239.4 184.0 %all-gather.8.cloned.1.call-start = ((), (), s32[]{:S(2)}) async-start(), calls=%async_computation.6 | async-start | bytes 2228224 | tf_op jit(solution)/shard_map/all_gather | solution.py:60
  319.8 156.5 %all-gather.10.cloned.1.call-start = ((), (), s32[]{:S(2)}) async-start(), calls=%async_computation.7 | async-start | bytes 2228224 | tf_op jit(solution)/shard_map/all_gather | solution.py:61
  327.0 20.1 %copy-start.2 = (bf16[256,256]{0,1:T(8,128)(2,1)S(1)}, bf16[256,256]{0,1:T(8,128)(2,1)}, u32[]{:S(2)}) copy-start(bf16[256,256]{0,1:T(8,128)(2,1)} %fusion.20) | copy-start | bytes 393220
  327.0 107.9 %all-to-all-start.2 = ((bf16[256,16,512]{2,0,1:T(8,128)(2,1)}), bf16[256,16,512]{2,0,1:T(8,128)(2,1)}, u32[]{:S(2)}, u32[]{:S(2)}) async-start(bf16[256,16,512]{2,0,1:T(8,128)(2,1)} %copy.81), calls=%async_computation.3 | async-start | bytes 8388608 | tf_op jit(solution)/shard_map/all_to_all | solution.py:57
  346.8 3.8 copy-start.3
  346.8 195.7 %reduce-scatter.2.cloned.1.call-start = ((), (), s32[]{:S(2)}) async-start(), calls=%async_computation.5 | async-start | bytes 6291456 | tf_op jit(solution)/shard_map/reduce_scatter | solution.py:51
  502.1 16.6 %copy-start = (bf16[512,32,128]{2,1,0:T(8,128)(2,1)S(1)}, bf16[512,32,128]{2,1,0:T(8,128)(2,1)}, u32[]{:S(2)}) copy-start(bf16[512,32,128]{2,1,0:T(8,128)(2,1)} %copy.83) | copy-start | bytes 12582916
Sparse Core Ops, SparseCore 0:
  239.8 58.0 all-gather.5
  319.9 103.3 all-gather.7
  426.1 50.1 all-gather.9
  479.0 53.4 reduce-scatter.1
where the time goes:
time: 552 us; the launch traced here: 549 us
  waiting for transfers between devices  247 us (45%)
  local copies, waits for them, and re-layouts  163 us (30%)
  matrix products  51.3 us (9%)
  starting transfers between devices  44.5 us (8%)
  blocking collectives  23.3 us (4%)
  between operations  13.9 us (3%)
  other arithmetic  5.91 us (1%)
    unnamed x18, local copies, waits for them, and re-layouts  75.5 us
    all_to_all x1, waiting for transfers between devices, per_device(): lax.all_to_all(gate_send, 'dp', split_axis=1, concat_axis=0, tiled=True)  72.6 us
    all_gather x1, waiting for transfers between devices, per_device(): lax.all_gather(gate_grad, 'dp', axis=0, tiled=True)  65.8 us
    all_gather x1, waiting for transfers between devices, per_device(): gathered = lax.all_gather(tokens, 'tensor', axis=1, tiled=True)  58.2 us
    all_gather x1, waiting for transfers between devices, per_device(): lax.all_gather(up_grad, 'dp', axis=0, tiled=True)  27.4 us
    all_gather x1, blocking collectives, per_device(): listed = lax.all_gather(active, 'dp', axis=0, tiled=True)  23.3 us
    reshape x1, local copies, waits for them, and re-layouts, per_device(): w_gate.reshape(rows_local, blocks, BLOCK)  19.9 us
    reshape x1, local copies, waits for them, and re-layouts, per_device(): w_up.reshape(rows_local, blocks, BLOCK)  19.9 us
  transfers between devices with their start and end apart: 7, of which 6 were waited for; matrix products, arithmetic and copies ran while one was open for 20% of the time, Pallas kernels for 0%

commit v1 on v0

--- a/solution.py
+++ b/solution.py
@@ -6,6 +6,19 @@
 BLOCK = 128
 TILE = 256
 CAP = 2
+
+
+def gather_around(x, axis, dim):
+    ways = lax.axis_size(axis)
+    up = [(d, (d + 1) % ways) for d in range(ways)]
+    down = [(d, (d - 1) % ways) for d in range(ways)]
+    earlier, later = ([x], [x])
+    for _ in range(ways // 2):
+        earlier.append(lax.ppermute(earlier[-1], axis, up))
+    for _ in range((ways - 1) // 2):
+        later.append(lax.ppermute(later[-1], axis, down))
+    line = jnp.concatenate([*earlier[::-1], *later[1:]], axis=dim)
+    return jnp.roll(line, (lax.axis_index(axis) - ways // 2) * x.shape[dim], axis=dim)
 
 
 def per_device(tokens, out_grad, active, w_gate, w_up):
@@ -57,7 +70,7 @@
     row_slices = lax.all_to_all(gathered, "dp", split_axis=1, concat_axis=0, tiled=True)
     slices_tiled = row_slices.reshape(peer_count * tiles_here, TILE, rows_local)
     gate_all, up_all = (
-        lax.all_gather(gate_grad, "dp", axis=0, tiled=True),
+        gather_around(gate_grad, "dp", 0),
         lax.all_gather(up_grad, "dp", axis=0, tiled=True),
     )
     gate_terms = jnp.einsum(

time: 552 us -> 583 us (1.056); the launches traced: 549 us -> 574 us
  starting transfers between devices: 44.5 us -> 80.7 us
  waiting for transfers between devices: 247 us -> 215 us
  local copies, waits for them, and re-layouts: 163 us -> 184 us
    ppermute x0 -> x15, waiting for transfers between devices: none -> 79.9 us  [the longest x8 79.8 us: gather_around(): earlier.append(lax.ppermute(earlier[-1], axis, up))]
    all_gather x1 -> x0, waiting for transfers between devices: 65.8 us -> none  [per_device(): lax.all_gather(gate_grad, 'dp', axis=0, tiled=True)]
    ppermute x0 -> x15, starting transfers between devices: none -> 32.3 us  [the longest x7 31.9 us: gather_around(): later.append(lax.ppermute(later[-1], axis, down))]
    all_gather x1, waiting for transfers between devices: 27.4 us -> 0.01 us  [per_device(): lax.all_gather(up_grad, 'dp', axis=0, tiled=True)]
    unnamed x18 -> x47, local copies, waits for them, and re-layouts: 75.5 us -> 95.9 us
    all_to_all x1, waiting for transfers between devices: 11.5 us -> 0.01 us  [per_device(): lax.all_to_all(gathered, 'dp', split_axis=1, concat_axis=0, tiled=True)]
    all_to_all x1, waiting for transfers between devices: 11.1 us -> 4.72 us  [per_device(): lax.all_to_all(up_send, 'dp', split_axis=1, concat_axis=0, tiled=True)]
  transfers between devices with their start and end apart: 7 -> 21, of which waited for: 6 -> 13; matrix products, arithmetic and copies ran while one was open for 20% -> 24% of each run, Pallas kernels for 0% -> 0%
where the time goes in v1:
time: 583 us; the launch traced here: 574 us
  waiting for transfers between devices  215 us (37%)
  local copies, waits for them, and re-layouts  184 us (32%)
  starting transfers between devices  80.7 us (14%)
  matrix products  50.7 us (9%)
  blocking collectives  23.3 us (4%)
  between operations  13.9 us (2%)
  other arithmetic  5.92 us (1%)
    unnamed x47, local copies, waits for them, and re-layouts  95.9 us
    ppermute x8, waiting for transfers between devices, gather_around(): earlier.append(lax.ppermute(earlier[-1], axis, up))  79.8 us
    all_to_all x1, waiting for transfers between devices, per_device(): lax.all_to_all(gate_send, 'dp', split_axis=1, concat_axis=0, tiled=True)  72.5 us
    all_gather x1, waiting for transfers between devices, per_device(): gathered = lax.all_gather(tokens, 'tensor', axis=1, tiled=True)  58.2 us
    ppermute x7, starting transfers between devices, gather_around(): later.append(lax.ppermute(later[-1], axis, down))  31.9 us
    all_to_all x1, starting transfers between devices, per_device(): lax.all_to_all(gathered, 'dp', split_axis=1, concat_axis=0, tiled=True)  23.9 us
    all_gather x1, blocking collectives, per_device(): listed = lax.all_gather(active, 'dp', axis=0, tiled=True)  23.3 us
    reshape x1, local copies, waits for them, and re-layouts, per_device(): w_gate.reshape(rows_local, blocks, BLOCK)  19.9 us
  transfers between devices with their start and end apart: 21, of which 13 were waited for; matrix products, arithmetic and copies ran while one was open for 24% of the time, Pallas kernels for 0%

profile of v1, /device:TPU:0, one launch (start us, length us, event | category | flops | bytes accessed | tf_op | source)
XLA Modules:
  0.0 573.7 jit_solution(8455184476655787836)
XLA Ops:
  7.2 23.3 %all_gather.9 = s32[16,1,2]{2,1,0:T(1,128)S(1)} all-gather(s32[1,1,2]{2,1,0:T(1,128)} %param.9), channel_id=1, replica_groups=mesh['dp'=16,'tensor'=2] {'dp'}, dimensions={0}, use_global_device_ids=true | all-gather | bytes 136 | tf_op jit(solution)/shard_map/all_gather | solution.py:31
  30.8 19.9 %copy.73 = bf16[512,14336]{0,1:T(8,128)(2,1)} copy(bf16[512,14336]{1,0:T(8,128)(2,1)} %param.10) | data formatting | bytes 29360128 | tf_op args[3]
  50.8 19.9 %copy.75 = bf16[512,112,128]{2,0,1:T(8,128)(2,1)} copy(bf16[512,112,128]{0,2,1:T(8,128)(2,1)} %bitcast.99) | data formatting | bytes 29360128 | tf_op jit(solution)/shard_map/reshape | solution.py:35
  70.7 19.9 %copy.67 = bf16[512,14336]{0,1:T(8,128)(2,1)} copy(bf16[512,14336]{1,0:T(8,128)(2,1)} %param.11) | data formatting | bytes 29360128 | tf_op args[4]
  90.6 19.9 %copy.69 = bf16[512,112,128]{2,0,1:T(8,128)(2,1)} copy(bf16[512,112,128]{0,2,1:T(8,128)(2,1)} %bitcast.100) | data formatting | bytes 29360128 | tf_op jit(solution)/shard_map/reshape | solution.py:38
  110.5 8.2 %gather_fusion.1 = bf16[32,512,128]{2,1,0:T(8,128)(2,1)} fusion(bf16[512,112,128]{2,0,1:T(8,128)(2,1)} %copy.75, s32[1024]{0:T(1024)S(1)} %pad_clamp_fusion), kind=kCustom, calls=%fused_computation.1.clone | custom fusion | bytes 8388736 | tf_op jit(solution)/shard_map/jit(_take)/gather | solution.py:35
  118.8 8.3 %gather_fusion = bf16[32,512,128]{2,1,0:T(8,128)(2,1)} fusion(bf16[512,112,128]{2,0,1:T(8,128)(2,1)} %copy.69, s32[1024]{0:T(1024)S(1)} %pad_clamp_fusion), kind=kCustom, calls=%fused_computation.clone | custom fusion | bytes 8388736 | tf_op jit(solution)/shard_map/jit(_take)/gather | solution.py:38
  127.0 5.2 select_bitcast_fusion.1
  135.0 4.6 all-to-all-start.1
  139.6 4.9 copy.97
  144.5 72.5 %all-to-all-done.1 = bf16[512,16,256]{2,0,1:T(8,128)(2,1)} async-done(((bf16[512,16,256]{2,0,1:T(8,128)(2,1)}), bf16[512,16,256]{2,0,1:T(8,128)(2,1)}, u32[]{:S(2)}, u32[]{:S(2)}) %all-to-all-start.1) | async-done | bytes 4194336 | tf_op jit(solution)/shard_map/all_to_all | solution.py:42
  217.1 19.8 %all-to-all-start = ((bf16[512,16,256]{2,0,1:T(8,128)(2,1)}), bf16[512,16,256]{2,0,1:T(8,128)(2,1)}, u32[]{:S(2)}, u32[]{:S(2)}) async-start(bf16[512,16,256]{2,0,1:T(8,128)(2,1)} %bitcast.106), calls=%async_computation | async-start | bytes 8388608 | tf_op jit(solution)/shard_map/all_to_all | solution.py:43
  239.7 58.2 %all-gather.4.cloned.1.call-done = bf16[256,8192]{0,1:T(8,128)(2,1)} async-done(((bf16[256,4096]{0,1:T(8,128)(2,1)}), bf16[256,8192]{0,1:T(8,128)(2,1)}) %all-gather.4.cloned.1.call-update) | async-done | bytes 4194320 | tf_op jit(solution)/shard_map/all_gather | solution.py:29
  297.9 5.4 fusion.21
  303.3 6.4 %copy.77 = bf16[256,16,512]{2,0,1:T(8,128)(2,1)} copy(bf16[256,16,512]{0,2,1:T(8,128)(2,1)} %bitcast.103) | data formatting | bytes 8388608 | tf_op jit(solution)/shard_map/all_to_all | solution.py:70
  309.7 4.7 all-to-all-done
  314.4 23.9 %all-to-all-start.2 = ((bf16[256,16,512]{2,0,1:T(8,128)(2,1)}), bf16[256,16,512]{2,0,1:T(8,128)(2,1)}, u32[]{:S(2)}, u32[]{:S(2)}) async-start(bf16[256,16,512]{2,0,1:T(8,128)(2,1)} %copy.77), calls=%async_computation.3 | async-start | bytes 8388608 | tf_op jit(solution)/shard_map/all_to_all | solution.py:70
  338.4 4.8 fusion.19
  346.8 5.7 fusion
  352.9 63.1 %collective-permute-done = bf16[1,256,256]{1,2,0:T(8,128)(2,1)S(1)} collective-permute-done((bf16[1,256,256]{1,2,0:T(8,128)(2,1)S(1)}, bf16[1,256,256]{1,2,0:T(8,128)(2,1)S(1)}, u32[]{:S(2)}, u32[]{:S(2)}) %collective-permute-start) | collective-permute-done | bytes 131104 | tf_op jit(solution)/shard_map/ppermute | solution.py:17
  430.4 4.6 collective-permute-start.10
  437.6 4.7 collective-permute-start.11
  444.8 4.6 collective-permute-start.12
  451.9 4.6 collective-permute-start.13
  487.3 6.1 %fusion.8 = bf16[16,256,512]{2,1,0:T(8,128)(2,1)} fusion(bf16[256,16,512]{2,0,1:T(8,128)(2,1)} %all-to-all-done.2, bf16[32,16,8,256]{3,2,1,0:T(8,128)(2,1)} %bitcast.114), kind=kOutput, calls=%fused_computation.17 | convolution fusion | flops 1075838976 | bytes 10485760 | tf_op jit(solution)/shard_map/tnr,tnc->rtc/dot_general | solution.py:79
  493.4 7.9 %copy.80 = bf16[512,32,128]{2,1,0:T(8,128)(2,1)} copy(bf16[512,32,128]{0,2,1:T(8,128)(2,1)} %bitcast.109) | data formatting | bytes 8388608 | tf_op jit(solution)/shard_map/reshape | solution.py:83
  501.3 6.1 %fusion.5 = bf16[16,256,512]{2,1,0:T(8,128)(2,1)} fusion(bf16[256,16,512]{2,0,1:T(8,128)(2,1)} %all-to-all-done.2, bf16[32,256,256]{1,2,0:T(8,128)(2,1)} %constant_dynamic-update-slice_fusion, s32[]{:T(128)S(6)} %select_n.21), kind=kOutput, calls=%fused_computation.16 | convolution fusion | flops 1075838976 | bytes 10485764 | tf_op jit(solution)/shard_map/tnr,tnc->rtc/dot_general | solution.py:76
  507.4 7.8 %copy.78 = bf16[512,32,128]{2,1,0:T(8,128)(2,1)} copy(bf16[512,32,128]{0,2,1:T(8,128)(2,1)} %bitcast.108) | data formatting | bytes 8388608 | tf_op jit(solution)/shard_map/reshape | solution.py:82
  515.2 11.7 %convolution_convert_fusion.1 = bf16[112,512,128]{2,0,1:T(8,128)(2,1)} fusion(bf16[512,32,128]{2,1,0:T(8,128)(2,1)} %copy.78, s32[32]{0:T(128)S(1)} %eq.18), kind=kOutput, calls=%fused_computation.6 | convolution fusion | flops 477105664 | bytes 18874496 | tf_op jit(solution)/shard_map/rsk,sb->rbk/dot_general | solution.py:87
  526.9 16.5 %copy.95 = bf16[64,8,112,128]{3,1,2,0:T(8,128)(2,1)} copy(bf16[64,8,112,128]{3,2,1,0:T(8,128)(2,1)} %bitcast.102) | data formatting | bytes 29360128
  543.4 7.4 %convolution_convert_fusion = bf16[112,512,128]{2,0,1:T(8,128)(2,1)} fusion(bf16[512,32,128]{2,1,0:T(8,128)(2,1)S(1)} %copy-done, s32[32]{0:T(128)S(1)} %eq.18), kind=kOutput, calls=%fused_computation.5 | convolution fusion | flops 477105664 | bytes 18874496 | tf_op jit(solution)/shard_map/rsk,sb->rbk/dot_general | solution.py:90
  550.8 16.3 %copy.94 = bf16[64,8,112,128]{3,1,2,0:T(8,128)(2,1)} copy(bf16[64,8,112,128]{3,2,1,0:T(8,128)(2,1)} %bitcast.101) | data formatting | bytes 29360128
  (92 shorter events, 62.7 us)
Async XLA Ops:
  135.0 82.0 %all-to-all-start.1 = ((bf16[512,16,256]{2,0,1:T(8,128)(2,1)}), bf16[512,16,256]{2,0,1:T(8,128)(2,1)}, u32[]{:S(2)}, u32[]{:S(2)}) async-start(bf16[512,16,256]{2,0,1:T(8,128)(2,1)} %bitcast.107), calls=%async_computation.1 | async-start | bytes 8388608 | tf_op jit(solution)/shard_map/all_to_all | solution.py:42
  217.1 19.9 %copy-start.1 = (bf16[256,4096]{1,0:T(8,128)(2,1)S(1)}, bf16[256,4096]{1,0:T(8,128)(2,1)}, u32[]{:S(2)}) copy-start(bf16[256,4096]{1,0:T(8,128)(2,1)} %param.7) | copy-start | bytes 6291460
  217.1 97.4 %all-to-all-start = ((bf16[512,16,256]{2,0,1:T(8,128)(2,1)}), bf16[512,16,256]{2,0,1:T(8,128)(2,1)}, u32[]{:S(2)}, u32[]{:S(2)}) async-start(bf16[512,16,256]{2,0,1:T(8,128)(2,1)} %bitcast.106), calls=%async_computation | async-start | bytes 8388608 | tf_op jit(solution)/shard_map/all_to_all | solution.py:43
  236.9 2.6 copy-start.3
  236.9 2.7 copy-start.4
  236.9 61.0 %all-gather.4.cloned.1.call-start = ((), (), s32[]{:S(2)}) async-start(), calls=%async_computation.4 | async-start | bytes 6291456 | tf_op jit(solution)/shard_map/all_gather | solution.py:29
  239.4 247.8 %all-gather.6.cloned.1.call-start = ((), (), s32[]{:S(2)}) async-start(), calls=%async_computation.6 | async-start | bytes 2228224 | tf_op jit(solution)/shard_map/all_gather | solution.py:74
  314.4 172.8 %all-to-all-start.2 = ((bf16[256,16,512]{2,0,1:T(8,128)(2,1)}), bf16[256,16,512]{2,0,1:T(8,128)(2,1)}, u32[]{:S(2)}, u32[]{:S(2)}) async-start(bf16[256,16,512]{2,0,1:T(8,128)(2,1)} %copy.77), calls=%async_computation.3 | async-start | bytes 8388608 | tf_op jit(solution)/shard_map/all_to_all | solution.py:70
  338.4 228.8 %reduce-scatter.2.cloned.1.call-start = ((), (), s32[]{:S(2)}) async-start(), calls=%async_computation.5 | async-start | bytes 6291456 | tf_op jit(solution)/shard_map/reduce_scatter | solution.py:64
  343.2 3.5 copy-start.2
  352.5 63.4 %collective-permute-start = (bf16[1,256,256]{1,2,0:T(8,128)(2,1)S(1)}, bf16[1,256,256]{1,2,0:T(8,128)(2,1)S(1)}, u32[]{:S(2)}, u32[]{:S(2)}) collective-permute-start(bf16[1,256,256]{1,2,0:T(8,128)(2,1)S(1)} %bitcast.112), channel_id=1, source_target_pairs={{0,2},{2,4},{4,6},{6,8},{8,10},{10,12},{12,14},{14,16},{16,18},{18... | collective-permute-start | bytes 393224 | tf_op jit(solution)/shard_map/ppermute | solution.py:17
  415.9 7.2 %collective-permute-start.1 = (bf16[1,256,256]{1,2,0:T(8,128)(2,1)S(1)}, bf16[1,256,256]{1,2,0:T(8,128)(2,1)S(1)}, u32[]{:S(2)}, u32[]{:S(2)}) collective-permute-start(bf16[1,256,256]{1,2,0:T(8,128)(2,1)S(1)} %collective-permute-done), channel_id=1, source_target_pairs={{0,2},{2,4},{4,6},{6,8},{8,10},{10,12},{12,14},{14,16},{16,18},{18... | collective-permute-start | bytes 393224 | tf_op jit(solution)/shard_map/ppermute | solution.py:17
  415.9 7.2 %collective-permute-start.8 = (bf16[1,256,256]{1,2,0:T(8,128)(2,1)S(1)}, bf16[1,256,256]{1,2,0:T(8,128)(2,1)S(1)}, u32[]{:S(2)}, u32[]{:S(2)}) collective-permute-start(bf16[1,256,256]{1,2,0:T(8,128)(2,1)S(1)} %bitcast.113), channel_id=1, source_target_pairs={{0,30},{2,0},{4,2},{6,4},{8,6},{10,8},{12,10},{14,12},{16,14},{18,... | collective-permute-start | bytes 393224 | tf_op jit(solution)/shard_map/ppermute | solution.py:19
  423.2 7.2 %collective-permute-start.2 = (bf16[1,256,256]{1,2,0:T(8,128)(2,1)S(1)}, bf16[1,256,256]{1,2,0:T(8,128)(2,1)S(1)}, u32[]{:S(2)}, u32[]{:S(2)}) collective-permute-start(bf16[1,256,256]{1,2,0:T(8,128)(2,1)S(1)} %collective-permute-done.1), channel_id=1, source_target_pairs={{0,2},{2,4},{4,6},{6,8},{8,10},{10,12},{12,14},{14,16},{16,18},{18... | collective-permute-start | bytes 393224 | tf_op jit(solution)/shard_map/ppermute | solution.py:17
  423.2 7.2 %collective-permute-start.9 = (bf16[1,256,256]{1,2,0:T(8,128)(2,1)S(1)}, bf16[1,256,256]{1,2,0:T(8,128)(2,1)S(1)}, u32[]{:S(2)}, u32[]{:S(2)}) collective-permute-start(bf16[1,256,256]{1,2,0:T(8,128)(2,1)S(1)} %collective-permute-done.8), channel_id=1, source_target_pairs={{0,30},{2,0},{4,2},{6,4},{8,6},{10,8},{12,10},{14,12},{16,14},{18,... | collective-permute-start | bytes 393224 | tf_op jit(solution)/shard_map/ppermute | solution.py:19
  430.4 7.2 %collective-permute-start.3 = (bf16[1,256,256]{1,2,0:T(8,128)(2,1)S(1)}, bf16[1,256,256]{1,2,0:T(8,128)(2,1)S(1)}, u32[]{:S(2)}, u32[]{:S(2)}) collective-permute-start(bf16[1,256,256]{1,2,0:T(8,128)(2,1)S(1)} %collective-permute-done.2), channel_id=1, source_target_pairs={{0,2},{2,4},{4,6},{6,8},{8,10},{10,12},{12,14},{14,16},{16,18},{18... | collective-permute-start | bytes 393224 | tf_op jit(solution)/shard_map/ppermute | solution.py:17
  430.4 7.2 %collective-permute-start.10 = (bf16[1,256,256]{1,2,0:T(8,128)(2,1)S(1)}, bf16[1,256,256]{1,2,0:T(8,128)(2,1)S(1)}, u32[]{:S(2)}, u32[]{:S(2)}) collective-permute-start(bf16[1,256,256]{1,2,0:T(8,128)(2,1)S(1)} %collective-permute-done.9), channel_id=1, source_target_pairs={{0,30},{2,0},{4,2},{6,4},{8,6},{10,8},{12,10},{14,12},{16,14},{18,... | collective-permute-start | bytes 393224 | tf_op jit(solution)/shard_map/ppermute | solution.py:19
  437.5 7.2 %collective-permute-start.4 = (bf16[1,256,256]{1,2,0:T(8,128)(2,1)S(1)}, bf16[1,256,256]{1,2,0:T(8,128)(2,1)S(1)}, u32[]{:S(2)}, u32[]{:S(2)}) collective-permute-start(bf16[1,256,256]{1,2,0:T(8,128)(2,1)S(1)} %collective-permute-done.3), channel_id=1, source_target_pairs={{0,2},{2,4},{4,6},{6,8},{8,10},{10,12},{12,14},{14,16},{16,18},{18... | collective-permute-start | bytes 393224 | tf_op jit(solution)/shard_map/ppermute | solution.py:17
  437.6 7.3 %collective-permute-start.11 = (bf16[1,256,256]{1,2,0:T(8,128)(2,1)S(1)}, bf16[1,256,256]{1,2,0:T(8,128)(2,1)S(1)}, u32[]{:S(2)}, u32[]{:S(2)}) collective-permute-start(bf16[1,256,256]{1,2,0:T(8,128)(2,1)S(1)} %collective-permute-done.10), channel_id=1, source_target_pairs={{0,30},{2,0},{4,2},{6,4},{8,6},{10,8},{12,10},{14,12},{16,14},{18,... | collective-permute-start | bytes 393224 | tf_op jit(solution)/shard_map/ppermute | solution.py:19
  444.7 7.1 %collective-permute-start.5 = (bf16[1,256,256]{1,2,0:T(8,128)(2,1)S(1)}, bf16[1,256,256]{1,2,0:T(8,128)(2,1)S(1)}, u32[]{:S(2)}, u32[]{:S(2)}) collective-permute-start(bf16[1,256,256]{1,2,0:T(8,128)(2,1)S(1)} %collective-permute-done.4), channel_id=1, source_target_pairs={{0,2},{2,4},{4,6},{6,8},{8,10},{10,12},{12,14},{14,16},{16,18},{18... | collective-permute-start | bytes 393224 | tf_op jit(solution)/shard_map/ppermute | solution.py:17
  444.8 7.1 %collective-permute-start.12 = (bf16[1,256,256]{1,2,0:T(8,128)(2,1)S(1)}, bf16[1,256,256]{1,2,0:T(8,128)(2,1)S(1)}, u32[]{:S(2)}, u32[]{:S(2)}) collective-permute-start(bf16[1,256,256]{1,2,0:T(8,128)(2,1)S(1)} %collective-permute-done.11), channel_id=1, source_target_pairs={{0,30},{2,0},{4,2},{6,4},{8,6},{10,8},{12,10},{14,12},{16,14},{18,... | collective-permute-start | bytes 393224 | tf_op jit(solution)/shard_map/ppermute | solution.py:19
  451.8 7.1 %collective-permute-start.6 = (bf16[1,256,256]{1,2,0:T(8,128)(2,1)S(1)}, bf16[1,256,256]{1,2,0:T(8,128)(2,1)S(1)}, u32[]{:S(2)}, u32[]{:S(2)}) collective-permute-start(bf16[1,256,256]{1,2,0:T(8,128)(2,1)S(1)} %collective-permute-done.5), channel_id=1, source_target_pairs={{0,2},{2,4},{4,6},{6,8},{8,10},{10,12},{12,14},{14,16},{16,18},{18... | collective-permute-start | bytes 393224 | tf_op jit(solution)/shard_map/ppermute | solution.py:17
  451.9 8.3 %collective-permute-start.13 = (bf16[1,256,256]{1,2,0:T(8,128)(2,1)S(1)}, bf16[1,256,256]{1,2,0:T(8,128)(2,1)S(1)}, u32[]{:S(2)}, u32[]{:S(2)}) collective-permute-start(bf16[1,256,256]{1,2,0:T(8,128)(2,1)S(1)} %collective-permute-done.12), channel_id=1, source_target_pairs={{0,30},{2,0},{4,2},{6,4},{8,6},{10,8},{12,10},{14,12},{16,14},{18,... | collective-permute-start | bytes 393224 | tf_op jit(solution)/shard_map/ppermute | solution.py:19
  458.9 7.1 %collective-permute-start.7 = (bf16[1,256,256]{1,2,0:T(8,128)(2,1)S(1)}, bf16[1,256,256]{1,2,0:T(8,128)(2,1)S(1)}, u32[]{:S(2)}, u32[]{:S(2)}) collective-permute-start(bf16[1,256,256]{1,2,0:T(8,128)(2,1)S(1)} %collective-permute-done.6), channel_id=1, source_target_pairs={{0,2},{2,4},{4,6},{6,8},{8,10},{10,12},{12,14},{14,16},{16,18},{18... | collective-permute-start | bytes 393224 | tf_op jit(solution)/shard_map/ppermute | solution.py:17
  460.2 15.8 %collective-permute-start.14 = (bf16[1,256,256]{1,2,0:T(8,128)(2,1)S(1)}, bf16[1,256,256]{1,2,0:T(8,128)(2,1)S(1)}, u32[]{:S(2)}, u32[]{:S(2)}) collective-permute-start(bf16[1,256,256]{1,2,0:T(8,128)(2,1)S(1)} %collective-permute-done.13), channel_id=1, source_target_pairs={{0,30},{2,0},{4,2},{6,4},{8,6},{10,8},{12,10},{14,12},{16,14},{18,... | collective-permute-start | bytes 393224 | tf_op jit(solution)/shard_map/ppermute | solution.py:19
  526.9 16.5 %copy-start = (bf16[512,32,128]{2,1,0:T(8,128)(2,1)S(1)}, bf16[512,32,128]{2,1,0:T(8,128)(2,1)}, u32[]{:S(2)}) copy-start(bf16[512,32,128]{2,1,0:T(8,128)(2,1)} %copy.80) | copy-start | bytes 12582916
Sparse Core Ops, SparseCore 0:
  239.8 58.0 all-gather.3
  303.4 69.8 all-gather.5
  376.2 53.3 reduce-scatter.1
